TPU v7x, 32 devices: a whole 2x2x4 slice. The times are simulated.
32 devices in a mesh: groups: 2 (over y), seq: 4 (over z), head: 4 (over x, core).
Axes of the slice: x: 2, y: 2, z: 4, core: 2. Of those that a mesh axis runs over, the one named last changes fastest.
Arguments:
- tokens: bfloat16 [4096, 4096], P(('groups', 'seq')), parts along dimension 0, may hold values from -24 to 24
- proj_weight: bfloat16 [3, 4096, 2048], P(None, 'seq', 'head'), may hold values from -1 to 1
- cluster_ids: int32 [16, 4096, 1], P('head', ('groups', 'seq')), parts along dimension 1, may hold values from 0 to 255; in each aligned block of 512 rows (0 to 511, 512 to 1023, ..., all dimensions but the last counted through in order) at most 4 rows name the same one
- centroids: float32 [32, 256, 128], P(('groups', 'head'), 'seq'), parts along dimension 0, may hold values from -3 to 3
Outputs:
- context: bfloat16 [4096, 2048], P(('groups', 'seq'), 'head'), parts along dimension 0
- new_centroids: float32 [32, 256, 128], P(('groups', 'head'), 'seq'), parts along dimension 0
There are 2 independent parts, one for each index of `groups`. A program takes and returns all parts, laid end to end along the dimension named above; an argument that names none is the same for every part. Nothing has to cross between parts.
Inputs may be any that keep to these rules, and one draw needn't show every extreme that they name: `cluster_ids`: for each head, no cluster is named by more than 4 of the 512 tokens of one aligned block (one index of seq); some blocks reach 4.
All inputs are finite; a program needn't handle non-finite values.
Results may differ from a plain program's by a relative error of at most 0.018.
Values may be sent and summed in bfloat16 or wider, within the bound.
A program may use at most 64 MiB of HBM per device.

v0:
```python
import jax
import jax.numpy as jnp
from jax import lax
from jax.sharding import PartitionSpec as P

HS = 128
CLUSTERS = 256
SLOTS = 4


def local(tokens, proj_weight, cluster_ids, centroids):
    owners = lax.axis_size("seq")
    local_rows = tokens.shape[0]
    columns = proj_weight.shape[2]
    head_count = columns // HS
    owned = CLUSTERS // owners
    capacity = owners * SLOTS
    score_scale = HS ** (-0.5)
    projected = jnp.einsum(
        "td,pdc->ptc",
        tokens,
        lax.all_gather(proj_weight, "seq", axis=1, tiled=True),
        preferred_element_type=jnp.float32,
    ).astype(jnp.bfloat16)
    per_head = projected.reshape(3, local_rows, head_count, HS).transpose(2, 1, 0, 3)
    packed = per_head.reshape(head_count, local_rows, 3 * HS)
    member = cluster_ids[:, :, 0]
    labels = jnp.arange(CLUSTERS, dtype=jnp.int32)
    onehot = (member[:, :, None] == labels[None, None, :]).astype(jnp.bfloat16)
    ordinal_rows = jnp.arange(local_rows, dtype=jnp.int32)
    earlier = (ordinal_rows[None, :] < ordinal_rows[:, None]).astype(jnp.bfloat16)
    before = jnp.einsum("ts,hsc->htc", earlier, onehot, preferred_element_type=jnp.float32)
    ranking = jnp.take_along_axis(before, member[:, :, None], axis=2)[:, :, 0].astype(jnp.int32)
    placed = member * SLOTS + ranking
    head_index = jnp.arange(head_count, dtype=jnp.int32)[:, None]
    outbox = (
        jnp.zeros((head_count, CLUSTERS * SLOTS, 3 * HS), jnp.bfloat16)
        .at[head_index, placed]
        .set(packed)
    )
    outbox = outbox.reshape(head_count, owners, owned * SLOTS, 3 * HS)
    local_counts = jnp.sum(onehot, axis=1, dtype=jnp.float32)
    tallies = local_counts.astype(jnp.int32).reshape(head_count, owners, owned)
    blocks = lax.all_to_all(outbox, "seq", split_axis=1, concat_axis=1, tiled=True)
    arrived = lax.all_to_all(tallies, "seq", split_axis=1, concat_axis=1, tiled=True)
    local_heads = blocks.shape[0]
    arranged = (
        blocks.reshape(local_heads, owners, owned, SLOTS, 3 * HS)
        .transpose(0, 2, 1, 3, 4)
        .reshape(local_heads, owned, capacity, 3 * HS)
    )
    filled = jnp.arange(SLOTS, dtype=jnp.int32)[None, None, None, :] < arrived[:, :, :, None]
    filled = filled.transpose(0, 2, 1, 3).reshape(local_heads, owned, capacity)
    queries = arranged[:, :, :, :HS]
    key_block = arranged[:, :, :, HS : 2 * HS]
    value_block = arranged[:, :, :, 2 * HS :]
    scores = (
        jnp.einsum("hcqd,hckd->hcqk", queries, key_block, preferred_element_type=jnp.float32)
        * score_scale
    )
    ordinal = jnp.arange(capacity, dtype=jnp.int32)
    causal = ordinal[None, None, None, :] <= ordinal[None, None, :, None]
    itself = ordinal[None, None, None, :] == ordinal[None, None, :, None]
    allowed = filled[:, :, None, :] & causal | itself
    scores = jnp.where(allowed, scores, -1e30)
    row_max = jnp.max(scores, axis=3, keepdims=True)
    raised = jnp.exp(scores - row_max)
    weights = (raised / jnp.sum(raised, axis=3, keepdims=True)).astype(jnp.bfloat16)
    attended = jnp.einsum(
        "hcqk,hckd->hcqd", weights, value_block, preferred_element_type=jnp.float32
    ).astype(jnp.bfloat16)
    attended = (
        attended.reshape(local_heads, owned, owners, SLOTS, HS)
        .transpose(0, 2, 1, 3, 4)
        .reshape(local_heads, owners, owned * SLOTS, HS)
    )
    returned = lax.all_to_all(attended, "seq", split_axis=1, concat_axis=1, tiled=True)
    key_sums = jnp.einsum(
        "hck,hckd->hcd", filled.astype(jnp.bfloat16), key_block, preferred_element_type=jnp.float32
    )
    counts = jnp.sum(filled, axis=2).astype(jnp.float32)
    exchanged = (returned, key_sums, counts)
    returned, key_sums, counts = exchanged
    gathered = returned.reshape(head_count, CLUSTERS * SLOTS, HS)
    mine = jax.vmap(lambda table, where: table[where])(gathered, placed)
    context = mine.transpose(1, 0, 2).reshape(local_rows, head_count * HS)
    updated = 0.25 * centroids + 0.75 * key_sums / jnp.maximum(counts, 1.0)[:, :, None]
    return (context, updated)


def solution(mesh):
    return jax.shard_map(
        local,
        mesh=mesh,
        in_specs=(
            P(("groups", "seq"), None),
            P(None, "seq", "head"),
            P("head", ("groups", "seq"), None),
            P(("groups", "head"), "seq", None),
        ),
        out_specs=(P(("groups", "seq"), "head"), P(("groups", "head"), "seq", None)),
        check_vma=False,
    )
```

profile of v0, /device:TPU:0, one launch (start us, length us, event | category | flops | bytes accessed | tf_op | source)
XLA Modules:
  0.0 396.1 jit_solution(17036133081253212412)
XLA Ops:
  7.2 4.7 %copy.40 = bf16[3,1024,512]{1,2,0:T(8,128)(2,1)} copy(bf16[3,1024,512]{2,1,0:T(8,128)(2,1)} %param.5) | data formatting | bytes 6291456 | tf_op args[1]
  13.7 6.3 %all-to-all-start = ((s32[4,1,256]{2,1,0:T(1,128)}), s32[4,1,256]{2,1,0:T(1,128)S(1)}, u32[]{:S(2)}, u32[]{:S(2)}) async-start(s32[4,1,256]{2,1,0:T(1,128)} %reshape.146), calls=%async_computation | async-start | bytes 8192 | tf_op jit(solution)/shard_map/all_to_all | solution.py:45
  20.1 0.8 fusion.8
  20.9 20.6 %gather_fusion = f32[2048]{0:T(1024)S(1)} fusion(f32[4,512,256]{1,2,0:T(8,128)S(1)} %fusion.8, s32[2048]{0:T(1024)S(1)} %bitcast.67), kind=kCustom, calls=%fused_computation | custom fusion | bytes 40960 | tf_op jit(solution)/shard_map/jit(take_along_axis)/gather | solution.py:33
  41.7 191.3 %all-gather.2.cloned.1.call-done = bf16[3,4096,512]{1,2,0:T(8,128)(2,1)} async-done(((bf16[3,1024,512]{1,2,0:T(8,128)(2,1)}), bf16[3,4096,512]{1,2,0:T(8,128)(2,1)}) %all-gather.2.cloned.1.call-update) | async-done | bytes 12582928 | tf_op jit(solution)/shard_map/all_gather | solution.py:22
  233.0 10.9 %fusion.5 = bf16[3,512,512]{2,1,0:T(8,128)(2,1)S(1)} fusion(bf16[3,4096,512]{1,2,0:T(8,128)(2,1)} %all-gather.2.cloned.1.call-done, bf16[512,4096]{1,0:T(8,128)(2,1)} %param.4), kind=kOutput, calls=%fused_computation.13 | convolution fusion | flops 6443237376 | bytes 18350080 | tf_op jit(solution)/shard_map/td,pdc->ptc/dot_general | solution.py:19
  243.9 1.2 copy.41
  245.6 1.6 copy.42
  247.2 10.9 %scatter_custom_fusion = bf16[4096,384]{1,0:T(8,128)(2,1)S(1)} fusion(s32[2048]{0:T(1024)S(1)} %bitcast.82, bf16[2048,384]{1,0:T(8,128)(2,1)} %copy.42, bf16[]{:T(256)} %constant.15.clone.1), kind=kCustom, calls=%fused_computation.15 | custom fusion | bytes 3146240
  258.1 2.0 copy.43
  260.1 3.9 all-to-all-start.1
  265.6 69.3 %all-to-all-done.1 = bf16[4,4,256,384]{3,2,0,1:T(8,128)(2,1)S(1)} async-done(((bf16[4,4,256,384]{3,2,0,1:T(8,128)(2,1)}), bf16[4,4,256,384]{3,2,0,1:T(8,128)(2,1)S(1)}, u32[]{:S(2)}, u32[]{:S(2)}) %all-to-all-start.1) | async-done | bytes 3145760 | tf_op jit(solution)/shard_map/all_to_all | solution.py:44
  334.9 2.4 copy.44
  337.3 1.6 copy.45
  338.9 2.4 reshape.108
  341.4 3.5 fusion.27
  344.9 1.7 convolution_convert_fusion
  347.1 1.1 copy.48
  348.2 3.6 all-to-all-start.2
  352.2 1.6 fusion.17
  353.9 0.8 divide_add_fusion
  354.6 22.5 %all-to-all-done.2 = bf16[4,4,256,128]{3,2,0,1:T(8,128)(2,1)S(1)} async-done(((bf16[4,4,256,128]{3,2,0,1:T(8,128)(2,1)}), bf16[4,4,256,128]{3,2,0,1:T(8,128)(2,1)S(1)}, u32[]{:S(2)}, u32[]{:S(2)}) %all-to-all-start.2) | async-done | bytes 1048608 | tf_op jit(solution)/shard_map/all_to_all | solution.py:77
  377.2 11.1 %gather_fusion.1 = bf16[2048,128]{1,0:T(8,128)(2,1)S(1)} fusion(bf16[4,1024,128]{2,1,0:T(8,128)(2,1)S(1)} %bitcast.68, s32[2048]{0:T(1024)S(1)} %bitcast.66), kind=kCustom, calls=%fused_computation.1 | custom fusion | bytes 1064960 | tf_op jit(solution)/shard_map/vmap()/gather | solution.py:85
  388.4 0.9 copy.66
  (48 shorter events, 5.0 us)
Async XLA Ops:
  7.2 225.8 %all-gather.2.cloned.1.call-start = ((), (), s32[]{:S(2)}) async-start(), calls=%async_computation.3 | async-start | bytes 15728640 | tf_op jit(solution)/shard_map/all_gather | solution.py:22
  11.9 0.7 copy-start.1
  13.7 246.4 %all-to-all-start = ((s32[4,1,256]{2,1,0:T(1,128)}), s32[4,1,256]{2,1,0:T(1,128)S(1)}, u32[]{:S(2)}, u32[]{:S(2)}) async-start(s32[4,1,256]{2,1,0:T(1,128)} %reshape.146), calls=%async_computation | async-start | bytes 8192 | tf_op jit(solution)/shard_map/all_to_all | solution.py:45
  20.8 20.6 %copy-start.2 = (s32[2]{0:T(128)S(1)}, s32[2]{0:T(128)}, u32[]{:S(2)}) copy-start(s32[2]{0:T(128)} %constant.42) | copy-start | bytes 28
  20.8 20.7 %copy-start.3 = (s32[2]{0:T(128)S(1)}, s32[2]{0:T(128)}, u32[]{:S(2)}) copy-start(s32[2]{0:T(128)} %constant.45) | copy-start | bytes 28
  260.1 74.8 %all-to-all-start.1 = ((bf16[4,4,256,384]{3,2,0,1:T(8,128)(2,1)}), bf16[4,4,256,384]{3,2,0,1:T(8,128)(2,1)S(1)}, u32[]{:S(2)}, u32[]{:S(2)}) async-start(bf16[4,4,256,384]{3,2,0,1:T(8,128)(2,1)} %copy.43), calls=%async_computation.1 | async-start | bytes 6291456 | tf_op jit(solution)/shard_map/all_to_all | solution.py:44
  348.2 5.7 %copy-start = (f32[4,64,128]{2,1,0:T(8,128)S(1)}, f32[4,64,128]{2,1,0:T(8,128)}, u32[]{:S(2)}) copy-start(f32[4,64,128]{2,1,0:T(8,128)} %param.7) | copy-start | bytes 393220
  348.2 28.9 %all-to-all-start.2 = ((bf16[4,4,256,128]{3,2,0,1:T(8,128)(2,1)}), bf16[4,4,256,128]{3,2,0,1:T(8,128)(2,1)S(1)}, u32[]{:S(2)}, u32[]{:S(2)}) async-start(bf16[4,4,256,128]{3,2,0,1:T(8,128)(2,1)} %copy.48), calls=%async_computation.2 | async-start | bytes 2097152 | tf_op jit(solution)/shard_map/all_to_all | solution.py:77
Sparse Core Ops, SparseCore 0:
  12.0 220.8 all-gather.1
where the time goes:
time: 397 us; the launch traced here: 396 us
  waiting for transfers between devices  283 us (71%)
  local copies, waits for them, and re-layouts  64.1 us (16%)
  matrix products  18.5 us (5%)
  between operations  14.3 us (4%)
  starting transfers between devices  13.9 us (4%)
    all_gather x1, waiting for transfers between devices, local(): lax.all_gather(proj_weight, 'seq', axis=1, tiled=True)  191 us
    all_to_all x1, waiting for transfers between devices, local(): lax.all_to_all(outbox, 'seq', split_axis=1, concat_axis=1, tiled=True)  69.3 us
    all_to_all x1, waiting for transfers between devices, local(): lax.all_to_all(attended, 'seq', split_axis=1, concat_axis=1, tiled=True)  22.5 us
    gather x2, local copies, waits for them, and re-layouts, local(): jnp.take_along_axis(before, member[:, :, None], axis=2)[:, :, 0]  20.6 us
    unnamed x18, local copies, waits for them, and re-layouts  17.5 us
    gather x1, local copies, waits for them, and re-layouts, local(): mine = jax.vmap(lambda table, where: table[where])(gathered, placed)  11.1 us
    dot_general x1, matrix products, local(): jnp.einsum('td,pdc->ptc', tokens, lax.all_gather(proj_weight, 'seq', axis...  10.9 us
  transfers between devices with their start and end apart: 4, of which 3 were waited for; matrix products, arithmetic and copies ran while one was open for 14% of the time, Pallas kernels for 0%

commit v1 on v0

--- a/solution.py
+++ b/solution.py
@@ -1,6 +1,10 @@
+import functools
+
 import jax
 import jax.numpy as jnp
 from jax import lax
+from jax.experimental import pallas as pl
+from jax.experimental.pallas import tpu as pltpu
 from jax.sharding import PartitionSpec as P
 
 HS = 128
@@ -8,7 +12,7 @@
 SLOTS = 4
 
 
-def local(tokens, proj_weight, cluster_ids, centroids):
+def general(tokens, proj_weight, cluster_ids, centroids):
     owners = lax.axis_size("seq")
     local_rows = tokens.shape[0]
     columns = proj_weight.shape[2]
@@ -88,6 +92,366 @@
     return (context, updated)
 
 
+MESH = pl.DeviceIdType.MESH
+PIECES = 4
+ROWS = 256
+QROWS = 128
+
+
+def kernel(
+    tok_hbm, w_hbm, ids_hbm, cent_ref, ctx_ref, new_ref,
+    tok, w, qkv, ids, ids_col, ctx_out, cent_out, cent_in,
+    local_sem, ids_send, ids_recv, wz_send, wz_recv, wy_send, wy_recv,
+    z_send, z_recv, x_send, x_recv, c_send, c_recv, ctx_send, ctx_recv, cent_send, cent_recv,
+):
+    g = lax.axis_index("groups")
+    z = lax.axis_index("seq")
+    h = lax.axis_index("head")
+    n = lax.axis_size("seq")
+    block = tok_hbm.shape[0]
+    depth = w_hbm.shape[1]
+    half = depth // 2
+    piece = block // PIECES // 4
+    group = block // PIECES
+    quarter = h
+    over_x = (g, z, lax.rem(h + 2, 4))
+    over_c = (g, z, h + 1 - 2 * lax.rem(h, 2))
+    over_y = (1 - g, z, h)
+
+    barrier = pltpu.get_barrier_semaphore()
+    for d in range(1, n):
+        pl.semaphore_signal(barrier, inc=1, device_id=(g, lax.rem(z + d, n), h), device_id_type=MESH)
+    for peer in (over_x, over_c, over_y):
+        pl.semaphore_signal(barrier, inc=1, device_id=peer, device_id_type=MESH)
+    pl.semaphore_wait(barrier, n + 2)
+
+    def remote(src, dst, send, recv, device):
+        return pltpu.make_async_remote_copy(
+            src_ref=src, dst_ref=dst, send_sem=send, recv_sem=recv, device_id=device, device_id_type=MESH
+        )
+
+    def col(j):
+        return pl.ds(pl.multiple_of(j * HS, HS), HS)
+
+    def rows_of(src, p, q):
+        return pl.ds(pl.multiple_of(src * block + p * group + q * piece, piece), piece)
+
+    def w_copy(d, j):
+        to = lax.rem(z + d, n)
+        return remote(
+            w_hbm.at[j, pl.ds(pl.multiple_of(g * half, half), half), col(to)],
+            w.at[pl.ds(pl.multiple_of(z * depth + g * half, half), half), pl.ds(j * HS, HS)],
+            wz_send.at[d - 1, j], wz_recv.at[d - 1, j], (g, to, h),
+        )
+
+    def w_arrived(d, j):
+        src = lax.rem(z - d + n, n)
+        part = w.at[pl.ds(pl.multiple_of(src * depth + g * half, half), half), pl.ds(j * HS, HS)]
+        return part
+
+    def ids_copy(d):
+        to = lax.rem(z + d, n)
+        return remote(
+            ids_hbm.at[to], ids.at[:, pl.ds(pl.multiple_of(z * block, block), block)],
+            ids_send.at[d - 1], ids_recv.at[d - 1], (g, to, h),
+        )
+
+    for j in range(3):
+        for d in range(1, n):
+            w_copy(d, j).start()
+    for d in range(1, n):
+        ids_copy(d).start()
+
+    def own_copy(p, up):
+        to = z + 1 if up else z - 1
+        return remote(
+            tok_hbm.at[pl.ds(pl.multiple_of(p * group + quarter * piece, piece), piece), :],
+            tok.at[rows_of(z, p, quarter), :],
+            z_send.at[1 if up else 0, z, p], z_recv.at[z, p], (g, to, h),
+        )
+
+    @pl.when(z < n - 1)
+    def _():
+        for p in range(PIECES):
+            own_copy(p, True).start()
+
+    @pl.when(z > 0)
+    def _():
+        for p in range(PIECES):
+            own_copy(p, False).start()
+
+    locals_ = [
+        pltpu.make_async_copy(tok_hbm, tok.at[pl.ds(pl.multiple_of(z * block, block), block), :], local_sem.at[0]),
+        pltpu.make_async_copy(ids_hbm.at[z], ids.at[:, pl.ds(pl.multiple_of(z * block, block), block)], local_sem.at[1]),
+    ]
+    for j in range(3):
+        locals_.append(
+            pltpu.make_async_copy(
+                w_hbm.at[j, :, col(z)],
+                w.at[pl.ds(pl.multiple_of(z * depth, depth), depth), pl.ds(j * HS, HS)],
+                local_sem.at[2 + j],
+            )
+        )
+    for copy in locals_:
+        copy.start()
+
+    def w_forward(d, j):
+        part = w_arrived(d, j)
+        return remote(part, part, wy_send.at[d - 1, j], wy_recv.at[d - 1, j], over_y)
+
+    for j in range(3):
+        for d in range(1, n):
+            w_copy(d, j).wait_recv()
+            w_forward(d, j).start()
+
+    def project(start):
+        rows = pl.ds(pl.multiple_of(start, ROWS), ROWS)
+        qkv[rows, :] = jnp.dot(tok[rows, :], w[...], preferred_element_type=jnp.float32).astype(jnp.bfloat16)
+
+    def source(s):
+        low = s + (s >= z).astype(jnp.int32)
+        high = n - 1 - (s + (s >= n - 1 - z).astype(jnp.int32))
+        return jnp.where(z < n // 2, low, high)
+
+    def split(t):
+        return source(t // PIECES), lax.rem(t, PIECES)
+
+    def along(src, p):
+        up = (src < z).astype(jnp.int32)
+        part = tok.at[rows_of(src, p, quarter), :]
+        return remote(part, part, z_send.at[up, src, p], z_recv.at[src, p], (g, z + 2 * up - 1, h))
+
+    def along_exists(src):
+        return jnp.where(src < z, z < n - 1, z > 0)
+
+    def across(src, p, q):
+        part = tok.at[rows_of(src, p, q), :]
+        return remote(part, part, x_send.at[src, p], x_recv.at[src, p], over_x)
+
+    def beside(src, p, which, q):
+        part = tok.at[rows_of(src, p, q), :]
+        return remote(part, part, c_send.at[which, src, p], c_recv.at[which, src, p], over_c)
+
+    other_x = lax.rem(h + 2, 4)
+    sib = h + 1 - 2 * lax.rem(h, 2)
+    sib_x = lax.rem(sib + 2, 4)
+    steps = (n - 1) * PIECES
+
+    def step(t, carry):
+        @pl.when(t < steps)
+        def _():
+            src, p = split(t)
+            along(src, p).wait_recv()
+
+            @pl.when(along_exists(src))
+            def _():
+                along(src, p).start()
+
+            across(src, p, quarter).start()
+            beside(src, p, 0, quarter).start()
+
+        @pl.when((t >= 1) & (t < steps + 1))
+        def _():
+            src, p = split(t - 1)
+            across(src, p, other_x).wait_recv()
+            beside(src, p, 1, other_x).start()
+
+        @pl.when(t >= 2)
+        def _():
+            src, p = split(t - 2)
+            beside(src, p, 0, sib).wait_recv()
+            beside(src, p, 1, sib_x).wait_recv()
+
+            @pl.when(lax.rem((p + 1) * group, ROWS) == 0)
+            def _():
+                project(src * block + (p + 1) * group - ROWS)
+
+        return carry
+
+    for j in range(3):
+        for d in range(1, n):
+            src = lax.rem(z - d + n, n)
+            part = w.at[pl.ds(pl.multiple_of(src * depth + (1 - g) * half, half), half), pl.ds(j * HS, HS)]
+            remote(part, part, wy_send.at[d - 1, j], wy_recv.at[d - 1, j], over_y).wait_recv()
+    for copy in locals_:
+        copy.wait()
+
+    def own_rows(i, carry):
+        project(z * block + i * ROWS)
+        return carry
+
+    lax.fori_loop(0, block // ROWS, own_rows, 0)
+    lax.fori_loop(0, steps + 2, step, 0)
+
+    for d in range(1, n):
+        ids_copy(d).wait_recv()
+    total = n * block
+    for i in range(total // 128):
+        row = ids[0:1, i * 128 : (i + 1) * 128].astype(jnp.float32)
+        ids_col[i * 128 : (i + 1) * 128, :] = jnp.broadcast_to(row, (128, 128)).T
+    scale = HS ** (-0.5)
+
+    def context_copy(i):
+        return remote(
+            ctx_out.at[pl.ds(i * block, block), :], ctx_ref.at[:, col(z)],
+            ctx_send.at[i], ctx_recv.at[z], (g, i, h),
+        )
+
+    def attend(i):
+        length = (i + 1) * block
+        key_ids = ids[0:1, 0:length].astype(jnp.float32)
+
+        def body(b, carry):
+            start = pl.multiple_of(i * block + b * QROWS, QROWS)
+            rows = pl.ds(start, QROWS)
+            scores = lax.dot_general(
+                qkv[rows, 0:HS], qkv[0:length, HS : 2 * HS], (((1,), (1,)), ((), ())),
+                preferred_element_type=jnp.float32,
+            ) * scale
+            at_query = start + lax.broadcasted_iota(jnp.int32, (QROWS, length), 0)
+            at_key = lax.broadcasted_iota(jnp.int32, (QROWS, length), 1)
+            allowed = (ids_col[rows, 0:1] == key_ids) & (at_key <= at_query)
+            scores = jnp.where(allowed, scores, -1e30)
+            raised = jnp.exp(scores - jnp.max(scores, axis=1, keepdims=True))
+            inverse = 1.0 / jnp.sum(raised, axis=1, keepdims=True)
+            weights = (raised * inverse).astype(jnp.bfloat16)
+            ctx_out[rows, :] = jnp.dot(
+                weights, qkv[0:length, 2 * HS : 3 * HS], preferred_element_type=jnp.float32
+            ).astype(jnp.bfloat16)
+            return carry
+
+        lax.fori_loop(0, block // QROWS, body, 0)
+
+        @pl.when(i != z)
+        def _():
+            context_copy(i).start()
+
+    clusters = cent_in.shape[1] * n
+    owned = cent_in.shape[1]
+    labels = lax.broadcasted_iota(jnp.int32, (clusters, total), 0)
+    member = (labels == ids[0:1, :]).astype(jnp.float32)
+    counts = jnp.sum(member, axis=1, keepdims=True)
+    key_sums = jnp.dot(
+        member.astype(jnp.bfloat16), qkv[:, HS : 2 * HS], preferred_element_type=jnp.float32
+    )
+    share = 0.75 * key_sums / jnp.maximum(counts, 1.0)
+    for i in range(n):
+        cent_out[i] = share[i * owned : (i + 1) * owned, :]
+
+    def cent_copy(i):
+        return remote(cent_out.at[i], cent_in.at[z], cent_send.at[i], cent_recv.at[z], (g, i, h))
+
+    for i in range(n):
+        @pl.when(i != z)
+        def _():
+            cent_copy(i).start()
+
+    for i in range(n):
+        attend(i)
+
+    ctx_ref[:, col(z)] = ctx_out[pl.ds(pl.multiple_of(z * block, block), block), :]
+    cent_in[z] = cent_out[z]
+
+    for i in range(n):
+        @pl.when(i != z)
+        def _():
+            remote(cent_out.at[i], cent_in.at[i], cent_send.at[i], cent_recv.at[i], (g, i, h)).wait_recv()
+    new_ref[...] = 0.25 * cent_ref[...] + cent_in[...]
+
+    for j in range(3):
+        for d in range(1, n):
+            w_copy(d, j).wait_send()
+            w_forward(d, j).wait_send()
+    for d in range(1, n):
+        ids_copy(d).wait_send()
+
+    @pl.when(z < n - 1)
+    def _():
+        for p in range(PIECES):
+            own_copy(p, True).wait_send()
+
+    @pl.when(z > 0)
+    def _():
+        for p in range(PIECES):
+            own_copy(p, False).wait_send()
+
+    def drain(t, carry):
+        src, p = split(t)
+
+        @pl.when(along_exists(src))
+        def _():
+            along(src, p).wait_send()
+
+        across(src, p, quarter).wait_send()
+        beside(src, p, 0, quarter).wait_send()
+        beside(src, p, 1, other_x).wait_send()
+        return carry
+
+    lax.fori_loop(0, steps, drain, 0)
+    for i in range(n):
+        @pl.when(i != z)
+        def _():
+            cent_copy(i).wait_send()
+            context_copy(i).wait_send()
+            remote(
+                ctx_out.at[pl.ds(i * block, block), :], ctx_ref.at[:, pl.ds(i * HS, HS)],
+                ctx_send.at[i], ctx_recv.at[i], (g, i, h),
+            ).wait_recv()
+
+
+def by_head(tokens, proj_weight, cluster_ids, centroids):
+    n = lax.axis_size("seq")
+    block, width = tokens.shape
+    heads = cluster_ids.shape[0]
+    owned = centroids.shape[1]
+    ids = jnp.broadcast_to(cluster_ids.reshape(heads, 1, block), (heads, 8, block))
+    dma = pltpu.SemaphoreType.DMA
+    return tuple(
+        pl.pallas_call(
+            kernel,
+            out_shape=(
+                jax.ShapeDtypeStruct((block, heads * HS), jnp.bfloat16),
+                jax.ShapeDtypeStruct((heads, owned, HS), jnp.float32),
+            ),
+            in_specs=[pl.BlockSpec(memory_space=pl.ANY)] * 3 + [pl.BlockSpec(memory_space=pltpu.VMEM)],
+            out_specs=(pl.BlockSpec(memory_space=pltpu.VMEM), pl.BlockSpec(memory_space=pltpu.VMEM)),
+            scratch_shapes=[
+                pltpu.VMEM((n * block, width), jnp.bfloat16),
+                pltpu.VMEM((width, 3 * HS), jnp.bfloat16),
+                pltpu.VMEM((n * block, 3 * HS), jnp.bfloat16),
+                pltpu.VMEM((8, n * block), jnp.int32),
+                pltpu.VMEM((n * block, HS), jnp.float32),
+                pltpu.VMEM((n * block, HS), jnp.bfloat16),
+                pltpu.VMEM((n, owned, HS), jnp.float32),
+                pltpu.VMEM((n, owned, HS), jnp.float32),
+                dma((5,)),
+                dma((n - 1,)), dma((n - 1,)),
+                dma((n - 1, 3)), dma((n - 1, 3)),
+                dma((n - 1, 3)), dma((n - 1, 3)),
+                dma((2, n, PIECES)), dma((n, PIECES)),
+                dma((n, PIECES)), dma((n, PIECES)),
+                dma((2, n, PIECES)), dma((2, n, PIECES)),
+                dma((n,)), dma((n,)),
+                dma((n,)), dma((n,)),
+            ],
+            compiler_params=pltpu.CompilerParams(
+                collective_id=0, has_side_effects=True, vmem_limit_bytes=58 << 20
+            ),
+        )(tokens, proj_weight, ids, centroids)
+    )
+
+
+def local(tokens, proj_weight, cluster_ids, centroids):
+    heads = cluster_ids.shape[0]
+    fits = (
+        lax.axis_size("seq") == heads
+        and lax.axis_size("head") == 4
+        and lax.axis_size("groups") == 2
+        and tokens.shape[0] % ROWS == 0
+    )
+    return (by_head if fits else general)(tokens, proj_weight, cluster_ids, centroids)
+
+
 def solution(mesh):
     return jax.shard_map(
         local,

time: 397 us -> 149 us (0.38)
  waiting for transfers between devices: 283 us -> 0 us
  Pallas kernels: 0 us -> 142 us
  local copies, waits for them, and re-layouts: 64.1 us -> 4.77 us
  matrix products: 18.5 us -> 0 us
  starting transfers between devices: 13.9 us -> 0 us
  between operations: 14.3 us -> 0.64 us
    all_gather x1 -> x0, waiting for transfers between devices: 191 us -> none  [local(): lax.all_gather(proj_weight, 'seq', axis=1, tiled=True)]
    pallas_call x0 -> x1, Pallas kernels: none -> 142 us  [by_head(): pl.pallas_call(kernel, out_shape=(jax.ShapeDtypeStruct((block, heads * HS...]
    all_to_all x3 -> x0, waiting for transfers between devices: 91.8 us -> none  [the longest x1 69.3 us: local(): lax.all_to_all(outbox, 'seq', split_axis=1, concat_axis=1, tiled=True)]
    gather x3 -> x0, local copies, waits for them, and re-layouts: 31.7 us -> none  [the longest x2 20.6 us: local(): jnp.take_along_axis(before, member[:, :, None], axis=2)[:, :, 0]]
    dot_general x4 -> x0, matrix products: 15.1 us -> none  [the longest x1 10.9 us: local(): jnp.einsum('td,pdc->ptc', tokens, lax.all_gather(proj_weight, 'seq', axis...]
    all_to_all x3 -> x0, starting transfers between devices: 13.9 us -> none  [the longest x1 6.35 us: local(): lax.all_to_all(tallies, 'seq', split_axis=1, concat_axis=1, tiled=True)]
    unnamed x18 -> x3, local copies, waits for them, and re-layouts: 17.5 us -> 4.14 us
    reshape x7 -> x0, local copies, waits for them, and re-layouts: 9.69 us -> none  [the longest x1 2.43 us: local(): arranged = blocks.reshape(local_heads, owners, owned, SLOTS, 3 * HS).tran...]
  transfers between devices with their start and end apart: 4 -> 0, of which waited for: 3 -> 0; matrix products, arithmetic and copies ran while one was open for 14% -> 0% of each run, Pallas kernels for 0% -> 0%
where the time goes in v1:
time: 149 us; the launch traced here: 147 us
  Pallas kernels  142 us (95%)
  local copies, waits for them, and re-layouts  4.77 us (3%)
    pallas_call x1, Pallas kernels, by_head(): pl.pallas_call(kernel, out_shape=(jax.ShapeDtypeStruct((block, heads * HS...  142 us
    unnamed x3, local copies, waits for them, and re-layouts  4.14 us

profile of v1, /device:TPU:0, one launch (start us, length us, event | category | flops | bytes accessed | tf_op | source)
XLA Modules:
  0.0 147.0 jit_solution(17823510094394849865)
XLA Ops:
  0.6 0.7 copy.8
  1.3 0.6 broadcast_in_dim.8.ids_hbm
  2.0 141.6 %shard_map.59 = (bf16[512,512]{1,0:T(8,128)(2,1)}, f32[4,64,128]{2,1,0:T(8,128)}) custom-call(bf16[512,4096]{1,0:T(8,128)(2,1)} %tok_hbm.1, bf16[3,1024,512]{2,1,0:T(8,128)(2,1)} %w_hbm.1, s32[4,8,512]{2,1,0:T(8,128)} %broadcast_in_dim.8.ids_hbm, f32[4,64,128]{2,1,0:T(8,128)} %cent_ref.1), custom_call_target="tpu_custom_call" | custom-call | tf_op jit(solution)/shard_map/pallas_call | solution.py:410
  143.6 1.9 %copy.11 = bf16[512,512]{1,0:T(8,128)(2,1)} copy(bf16[512,512]{1,0:T(8,128)(2,1)} %get-tuple-element.4) | data formatting | bytes 1048576
  145.4 1.6 %copy.12 = f32[4,64,128]{2,1,0:T(8,128)} copy(f32[4,64,128]{2,1,0:T(8,128)} %get-tuple-element.5) | data formatting | bytes 262144

commit v2 on v1

--- a/solution.py
+++ b/solution.py
@@ -100,7 +100,7 @@
 
 def kernel(
     tok_hbm, w_hbm, ids_hbm, cent_ref, ctx_ref, new_ref,
-    tok, w, qkv, ids, ids_col, ctx_out, cent_out, cent_in,
+    tok, w, qkv, ids, ids_col, member, counts, ctx_out, cent_out, cent_in,
     local_sem, ids_send, ids_recv, wz_send, wz_recv, wy_send, wy_recv,
     z_send, z_recv, x_send, x_recv, c_send, c_recv, ctx_send, ctx_recv, cent_send, cent_recv,
 ):
@@ -156,9 +156,6 @@
             ids_send.at[d - 1], ids_recv.at[d - 1], (g, to, h),
         )
 
-    for j in range(3):
-        for d in range(1, n):
-            w_copy(d, j).start()
     for d in range(1, n):
         ids_copy(d).start()
 
@@ -170,15 +167,17 @@
             z_send.at[1 if up else 0, z, p], z_recv.at[z, p], (g, to, h),
         )
 
-    @pl.when(z < n - 1)
-    def _():
+    def own_start(up):
         for p in range(PIECES):
-            own_copy(p, True).start()
-
-    @pl.when(z > 0)
-    def _():
-        for p in range(PIECES):
-            own_copy(p, False).start()
+            own_copy(p, up).start()
+
+    pl.when(z == 1)(lambda: own_start(False))
+    pl.when(z == n - 2)(lambda: own_start(True))
+    for j in range(3):
+        for d in range(1, n):
+            w_copy(d, j).start()
+    pl.when((z != 1) & (z < n - 2))(lambda: own_start(True))
+    pl.when(z > 1)(lambda: own_start(False))
 
     locals_ = [
         pltpu.make_async_copy(tok_hbm, tok.at[pl.ds(pl.multiple_of(z * block, block), block), :], local_sem.at[0]),
@@ -199,7 +198,7 @@
         part = w_arrived(d, j)
         return remote(part, part, wy_send.at[d - 1, j], wy_recv.at[d - 1, j], over_y)
 
-    for j in range(3):
+    def w_step(j):
         for d in range(1, n):
             w_copy(d, j).wait_recv()
             w_forward(d, j).start()
@@ -210,7 +209,7 @@
 
     def source(s):
         low = s + (s >= z).astype(jnp.int32)
-        high = n - 1 - (s + (s >= n - 1 - z).astype(jnp.int32))
+        high = jnp.where(s == 0, 2 * n - 3 - z, s - 1)
         return jnp.where(z < n // 2, low, high)
 
     def split(t):
@@ -237,58 +236,85 @@
     sib_x = lax.rem(sib + 2, 4)
     steps = (n - 1) * PIECES
 
-    def step(t, carry):
-        @pl.when(t < steps)
-        def _():
-            src, p = split(t)
-            along(src, p).wait_recv()
-
-            @pl.when(along_exists(src))
-            def _():
-                along(src, p).start()
-
-            across(src, p, quarter).start()
-            beside(src, p, 0, quarter).start()
-
-        @pl.when((t >= 1) & (t < steps + 1))
-        def _():
-            src, p = split(t - 1)
-            across(src, p, other_x).wait_recv()
-            beside(src, p, 1, other_x).start()
-
-        @pl.when(t >= 2)
-        def _():
-            src, p = split(t - 2)
-            beside(src, p, 0, sib).wait_recv()
-            beside(src, p, 1, sib_x).wait_recv()
-
-            @pl.when(lax.rem((p + 1) * group, ROWS) == 0)
-            def _():
-                project(src * block + (p + 1) * group - ROWS)
+    inner = (z > 0) & (z < n - 1)
+
+    def carry_on(t):
+        src, p = split(t)
+        along(src, p).wait_recv()
+
+        @pl.when(along_exists(src))
+        def _():
+            along(src, p).start()
+
+        across(src, p, quarter).start()
+        beside(src, p, 0, quarter).start()
+
+    def hand_over(t):
+        src, p = split(t)
+        across(src, p, other_x).wait_recv()
+        beside(src, p, 1, other_x).start()
+
+    def complete(t):
+        src, p = split(t)
+        beside(src, p, 0, sib).wait_recv()
+        beside(src, p, 1, sib_x).wait_recv()
+        return src, p
+
+    for d in range(1, n):
+        ids_copy(d).wait_recv()
+    for copy in locals_[:2]:
+        copy.wait()
+    total = n * block
+    for i in range(total // 128):
+        row = ids[0:1, i * 128 : (i + 1) * 128].astype(jnp.float32)
+        ids_col[i * 128 : (i + 1) * 128, :] = jnp.broadcast_to(row, (128, 128)).T
+    owned = cent_in.shape[1]
+    clusters = owned * n
+    labels = lax.broadcasted_iota(jnp.int32, (clusters, total), 0)
+    named = (labels == ids[0:1, :]).astype(jnp.float32)
+    counts[...] = jnp.broadcast_to(jnp.sum(named, axis=1, keepdims=True), counts.shape)
+    member[...] = named.astype(jnp.bfloat16)
+
+    for t in range(PIECES):
+        if t < 3:
+            pl.when(inner)(lambda: w_step(t))
+        carry_on(t)
+        if t < 3:
+            pl.when(~inner)(lambda: w_step(t))
+        if t >= 1:
+            hand_over(t - 1)
+        if t >= 2:
+            complete(t - 2)
+
+    pl.when(z == 1)(lambda: own_start(True))
+
+    def rest(t, carry):
+        pl.when(t < steps)(lambda: carry_on(t))
+        pl.when(t < steps + 1)(lambda: hand_over(t - 1))
+        src, p = complete(t - 2)
+
+        @pl.when((t >= PIECES + 2) & (lax.rem((p + 1) * group, ROWS) == 0))
+        def _():
+            project(src * block + (p + 1) * group - ROWS)
 
         return carry
+
+    lax.fori_loop(PIECES, PIECES + 2, rest, 0)
 
     for j in range(3):
         for d in range(1, n):
             src = lax.rem(z - d + n, n)
             part = w.at[pl.ds(pl.multiple_of(src * depth + (1 - g) * half, half), half), pl.ds(j * HS, HS)]
             remote(part, part, wy_send.at[d - 1, j], wy_recv.at[d - 1, j], over_y).wait_recv()
-    for copy in locals_:
+    for copy in locals_[2:]:
         copy.wait()
 
-    def own_rows(i, carry):
-        project(z * block + i * ROWS)
+    def early_rows(i, carry):
+        which = jnp.where(i < block // ROWS, z, source(0))
+        project(which * block + lax.rem(i, block // ROWS) * ROWS)
         return carry
 
-    lax.fori_loop(0, block // ROWS, own_rows, 0)
-    lax.fori_loop(0, steps + 2, step, 0)
-
-    for d in range(1, n):
-        ids_copy(d).wait_recv()
-    total = n * block
-    for i in range(total // 128):
-        row = ids[0:1, i * 128 : (i + 1) * 128].astype(jnp.float32)
-        ids_col[i * 128 : (i + 1) * 128, :] = jnp.broadcast_to(row, (128, 128)).T
+    lax.fori_loop(0, 2 * (block // ROWS), early_rows, 0)
     scale = HS ** (-0.5)
 
     def context_copy(i):
@@ -326,15 +352,20 @@
         def _():
             context_copy(i).start()
 
-    clusters = cent_in.shape[1] * n
-    owned = cent_in.shape[1]
-    labels = lax.broadcasted_iota(jnp.int32, (clusters, total), 0)
-    member = (labels == ids[0:1, :]).astype(jnp.float32)
-    counts = jnp.sum(member, axis=1, keepdims=True)
+    lax.fori_loop(PIECES + 2, 2 * PIECES + 2, rest, 0)
+    attend(0)
+
+    @pl.when(z < n // 2)
+    def _():
+        for i in range(1, n - 1):
+            attend(i)
+
+    lax.fori_loop(2 * PIECES + 2, steps + 2, rest, 0)
+
     key_sums = jnp.dot(
-        member.astype(jnp.bfloat16), qkv[:, HS : 2 * HS], preferred_element_type=jnp.float32
-    )
-    share = 0.75 * key_sums / jnp.maximum(counts, 1.0)
+        member[...], qkv[:, HS : 2 * HS], preferred_element_type=jnp.float32
+    )
+    share = 0.75 * key_sums / jnp.maximum(counts[...], 1.0)
     for i in range(n):
         cent_out[i] = share[i * owned : (i + 1) * owned, :]
 
@@ -346,8 +377,12 @@
         def _():
             cent_copy(i).start()
 
-    for i in range(n):
-        attend(i)
+    @pl.when(z >= n // 2)
+    def _():
+        for i in range(1, n - 1):
+            attend(i)
+
+    attend(n - 1)
 
     ctx_ref[:, col(z)] = ctx_out[pl.ds(pl.multiple_of(z * block, block), block), :]
     cent_in[z] = cent_out[z]
@@ -421,6 +456,8 @@
                 pltpu.VMEM((n * block, 3 * HS), jnp.bfloat16),
                 pltpu.VMEM((8, n * block), jnp.int32),
                 pltpu.VMEM((n * block, HS), jnp.float32),
+                pltpu.VMEM((n * owned, n * block), jnp.bfloat16),
+                pltpu.VMEM((n * owned, HS), jnp.float32),
                 pltpu.VMEM((n * block, HS), jnp.bfloat16),
                 pltpu.VMEM((n, owned, HS), jnp.float32),
                 pltpu.VMEM((n, owned, HS), jnp.float32),
@@ -444,7 +481,7 @@
 def local(tokens, proj_weight, cluster_ids, centroids):
     heads = cluster_ids.shape[0]
     fits = (
-        lax.axis_size("seq") == heads
+        lax.axis_size("seq") == heads == 4
         and lax.axis_size("head") == 4
         and lax.axis_size("groups") == 2
         and tokens.shape[0] % ROWS == 0

time: 149 us -> 141 us (0.946)
  Pallas kernels: 142 us -> 135 us
    pallas_call x1, Pallas kernels: 142 us -> 135 us  [by_head(): pl.pallas_call(kernel, out_shape=(jax.ShapeDtypeStruct((block, heads * HS...]
where the time goes in v2:
time: 141 us; the launch traced here: 140 us
  Pallas kernels  135 us (96%)
  local copies, waits for them, and re-layouts  4.77 us (3%)
    pallas_call x1, Pallas kernels, by_head(): pl.pallas_call(kernel, out_shape=(jax.ShapeDtypeStruct((block, heads * HS...  135 us
    unnamed x3, local copies, waits for them, and re-layouts  4.14 us

profile of v2, /device:TPU:0, one launch (start us, length us, event | category | flops | bytes accessed | tf_op | source)
XLA Modules:
  0.0 140.5 jit_solution(4306912763612438752)
XLA Ops:
  0.6 0.7 copy.8
  1.3 0.6 broadcast_in_dim.8.ids_hbm
  2.0 135.1 %shard_map.59 = (bf16[512,512]{1,0:T(8,128)(2,1)}, f32[4,64,128]{2,1,0:T(8,128)}) custom-call(bf16[512,4096]{1,0:T(8,128)(2,1)} %tok_hbm.1, bf16[3,1024,512]{2,1,0:T(8,128)(2,1)} %w_hbm.1, s32[4,8,512]{2,1,0:T(8,128)} %broadcast_in_dim.8.ids_hbm, f32[4,64,128]{2,1,0:T(8,128)} %cent_ref.1), custom_call_target="tpu_custom_call" | custom-call | tf_op jit(solution)/shard_map/pallas_call | solution.py:445
  137.0 1.9 %copy.11 = bf16[512,512]{1,0:T(8,128)(2,1)} copy(bf16[512,512]{1,0:T(8,128)(2,1)} %get-tuple-element.4) | data formatting | bytes 1048576
  138.9 1.6 %copy.12 = f32[4,64,128]{2,1,0:T(8,128)} copy(f32[4,64,128]{2,1,0:T(8,128)} %get-tuple-element.5) | data formatting | bytes 262144

commit v3 on v2

--- a/solution.py
+++ b/solution.py
@@ -95,11 +95,11 @@
 MESH = pl.DeviceIdType.MESH
 PIECES = 4
 ROWS = 256
-QROWS = 128
+QROWS = 256
 
 
 def kernel(
-    tok_hbm, w_hbm, ids_hbm, cent_ref, ctx_ref, new_ref,
+    tok_hbm, w_hbm, ids_hbm, ctx_ref, new_ref,
     tok, w, qkv, ids, ids_col, member, counts, ctx_out, cent_out, cent_in,
     local_sem, ids_send, ids_recv, wz_send, wz_recv, wy_send, wy_recv,
     z_send, z_recv, x_send, x_recv, c_send, c_recv, ctx_send, ctx_recv, cent_send, cent_recv,
@@ -152,7 +152,7 @@
     def ids_copy(d):
         to = lax.rem(z + d, n)
         return remote(
-            ids_hbm.at[to], ids.at[:, pl.ds(pl.multiple_of(z * block, block), block)],
+            ids_hbm.at[to], ids.at[0:1, pl.ds(pl.multiple_of(z * block, block), block)],
             ids_send.at[d - 1], ids_recv.at[d - 1], (g, to, h),
         )
 
@@ -171,17 +171,19 @@
         for p in range(PIECES):
             own_copy(p, up).start()
 
-    pl.when(z == 1)(lambda: own_start(False))
-    pl.when(z == n - 2)(lambda: own_start(True))
-    for j in range(3):
-        for d in range(1, n):
-            w_copy(d, j).start()
+    for p in range(max(3, PIECES)):
+        if p < PIECES:
+            pl.when(z == 1)(lambda: own_copy(p, False).start())
+            pl.when(z == n - 2)(lambda: own_copy(p, True).start())
+        if p < 3:
+            for d in range(1, n):
+                w_copy(d, p).start()
     pl.when((z != 1) & (z < n - 2))(lambda: own_start(True))
     pl.when(z > 1)(lambda: own_start(False))
 
     locals_ = [
         pltpu.make_async_copy(tok_hbm, tok.at[pl.ds(pl.multiple_of(z * block, block), block), :], local_sem.at[0]),
-        pltpu.make_async_copy(ids_hbm.at[z], ids.at[:, pl.ds(pl.multiple_of(z * block, block), block)], local_sem.at[1]),
+        pltpu.make_async_copy(ids_hbm.at[z], ids.at[0:1, pl.ds(pl.multiple_of(z * block, block), block)], local_sem.at[1]),
     ]
     for j in range(3):
         locals_.append(
@@ -275,15 +277,16 @@
     counts[...] = jnp.broadcast_to(jnp.sum(named, axis=1, keepdims=True), counts.shape)
     member[...] = named.astype(jnp.bfloat16)
 
-    for t in range(PIECES):
+    for t in range(max(3, PIECES)):
         if t < 3:
             pl.when(inner)(lambda: w_step(t))
-        carry_on(t)
+        if t < PIECES:
+            carry_on(t)
         if t < 3:
             pl.when(~inner)(lambda: w_step(t))
-        if t >= 1:
+        if 1 <= t < PIECES:
             hand_over(t - 1)
-        if t >= 2:
+        if 2 <= t < PIECES:
             complete(t - 2)
 
     pl.when(z == 1)(lambda: own_start(True))
@@ -391,7 +394,7 @@
         @pl.when(i != z)
         def _():
             remote(cent_out.at[i], cent_in.at[i], cent_send.at[i], cent_recv.at[i], (g, i, h)).wait_recv()
-    new_ref[...] = 0.25 * cent_ref[...] + cent_in[...]
+    new_ref[...] = cent_in[...]
 
     for j in range(3):
         for d in range(1, n):
@@ -434,21 +437,26 @@
             ).wait_recv()
 
 
+def finish(context_ref, share_ref, cent_ref, ctx_ref, new_ref):
+    ctx_ref[...] = context_ref[...]
+    new_ref[...] = 0.25 * cent_ref[...] + share_ref[...]
+
+
 def by_head(tokens, proj_weight, cluster_ids, centroids):
     n = lax.axis_size("seq")
     block, width = tokens.shape
     heads = cluster_ids.shape[0]
     owned = centroids.shape[1]
-    ids = jnp.broadcast_to(cluster_ids.reshape(heads, 1, block), (heads, 8, block))
+    ids = cluster_ids.reshape(heads, 1, block)
     dma = pltpu.SemaphoreType.DMA
-    return tuple(
+    context, share = (
         pl.pallas_call(
             kernel,
             out_shape=(
                 jax.ShapeDtypeStruct((block, heads * HS), jnp.bfloat16),
                 jax.ShapeDtypeStruct((heads, owned, HS), jnp.float32),
             ),
-            in_specs=[pl.BlockSpec(memory_space=pl.ANY)] * 3 + [pl.BlockSpec(memory_space=pltpu.VMEM)],
+            in_specs=[pl.BlockSpec(memory_space=pl.ANY)] * 3,
             out_specs=(pl.BlockSpec(memory_space=pltpu.VMEM), pl.BlockSpec(memory_space=pltpu.VMEM)),
             scratch_shapes=[
                 pltpu.VMEM((n * block, width), jnp.bfloat16),
@@ -474,7 +482,17 @@
             compiler_params=pltpu.CompilerParams(
                 collective_id=0, has_side_effects=True, vmem_limit_bytes=58 << 20
             ),
-        )(tokens, proj_weight, ids, centroids)
+        )(tokens, proj_weight, ids)
+    )
+    return tuple(
+        pl.pallas_call(
+            finish,
+            out_shape=(
+                jax.ShapeDtypeStruct(context.shape, context.dtype),
+                jax.ShapeDtypeStruct(centroids.shape, centroids.dtype),
+            ),
+            compiler_params=pltpu.CompilerParams(vmem_limit_bytes=8 << 20),
+        )(context, share, centroids)
     )
 
 

time: 141 us -> 136 us (0.965)
  local copies, waits for them, and re-layouts: 4.77 us -> 1.94 us
  Pallas kernels: 135 us -> 133 us
    pallas_call x1, Pallas kernels: 135 us -> 132 us  [by_head(): pl.pallas_call(kernel, out_shape=(jax.ShapeDtypeStruct((block, heads * HS...]
    unnamed x3 -> x6, local copies, waits for them, and re-layouts: 4.14 us -> 1.94 us
where the time goes in v3:
time: 136 us; the launch traced here: 135 us
  Pallas kernels  133 us (98%)
  local copies, waits for them, and re-layouts  1.94 us (1%)
    pallas_call x1, Pallas kernels, by_head(): pl.pallas_call(kernel, out_shape=(jax.ShapeDtypeStruct((block, heads * HS...  132 us

profile of v3, /device:TPU:0, one launch (start us, length us, event | category | flops | bytes accessed | tf_op | source)
XLA Modules:
  0.0 135.2 jit_solution(14352207788470193169)
XLA Ops:
  0.6 0.0 copy-start.1
  0.6 131.7 %shard_map.59 = (bf16[512,512]{1,0:T(8,128)(2,1)}, f32[4,64,128]{2,1,0:T(8,128)}) custom-call(bf16[512,4096]{1,0:T(8,128)(2,1)} %tok_hbm.1, bf16[3,1024,512]{2,1,0:T(8,128)(2,1)} %w_hbm.1, s32[4,1,512]{2,1,0:T(1,128)} %bitcast.1), custom_call_target="tpu_custom_call" | custom-call | tf_op jit(solution)/shard_map/pallas_call | solution.py:453
  132.4 0.0 copy-done.1
  132.4 0.0 copy-start
  132.4 1.0 copy-done
  133.4 0.0 copy-start.2
  133.4 0.9 copy-done.2
  134.3 0.9 shard_map.60
Async XLA Ops:
  0.6 131.7 %copy-start.1 = (f32[4,64,128]{2,1,0:T(8,128)S(1)}, f32[4,64,128]{2,1,0:T(8,128)}, u32[]{:S(2)}) copy-start(f32[4,64,128]{2,1,0:T(8,128)} %cent_ref.1) | copy-start | bytes 393220
  132.4 1.0 copy-start
  133.4 0.9 copy-start.2
